TPU v7x, 256 devices: a whole 4x4x8 slice. The times are simulated.
256 devices in a mesh: seq: 64 (over y_hi, z, x), fsdp: 4 (over y_lo, core).
Axes of the slice: x: 4, y: 4 (y_hi: 2, y_lo: 2; y = y_hi * 2 + y_lo), z: 8, core: 2. Of those that a mesh axis runs over, the one named last changes fastest.
Arguments:
- image_query: bfloat16 [4, 16384, 1536], P('fsdp', 'seq'), may hold values from -6 to 6
- image_key: bfloat16 [4, 16384, 1536], P('fsdp', 'seq'), may hold values from -6 to 6
- image_value: bfloat16 [4, 16384, 1536], P('fsdp', 'seq'), may hold values from -6 to 6
- text_key: bfloat16 [4, 512, 1536], P('fsdp'), may hold values from -6 to 6
- text_value: bfloat16 [4, 512, 1536], P('fsdp'), may hold values from -6 to 6
- out_weight: bfloat16 [1536, 1536], P('fsdp'), may hold values from -0.15625 to 0.15625
- cotangent: bfloat16 [4, 16384, 1536], P('fsdp', 'seq'), may hold values from -16 to 16
Outputs:
- image_out: bfloat16 [4, 16384, 1536], P('fsdp', 'seq')
- grad_query: bfloat16 [4, 16384, 1536], P('fsdp', 'seq')
- grad_key: bfloat16 [4, 16384, 1536], P('fsdp', 'seq')
- grad_value: bfloat16 [4, 16384, 1536], P('fsdp', 'seq')
- grad_weight: float32 [1536, 1536], P(('fsdp', 'seq'))
All inputs are finite; a program needn't handle non-finite values.
Results may differ from a plain program's by a relative error of at most 0.0095.
Values may be sent and summed in bfloat16 or wider, within the bound.
A program may use at most 128 MiB of HBM per device.

v0:
```python
import math

import jax
import jax.numpy as jnp
from jax import lax
from jax.sharding import PartitionSpec as P

HEAD_DIM = 128
STEPS = 4


def from_behind(block, axis, distance):
    devices = range(lax.axis_size(axis))
    route = [((i - distance) % len(devices), i) for i in devices]
    return lax.ppermute(block, axis, route)


def head_pass(inputs):
    head_query, head_key, head_value, head_grad = inputs
    scaling = 1.0 / math.sqrt(head_query.shape[1])
    scores = (
        lax.dot_general(
            head_query, head_key, (((1,), (1,)), ((), ())), preferred_element_type=jnp.float32
        )
        * scaling
    )
    row_peak = jnp.max(scores, axis=1, keepdims=True)
    shifted = jnp.exp(scores - row_peak)
    softmax = shifted / jnp.sum(shifted, axis=1, keepdims=True)
    prob_low = softmax.astype(jnp.bfloat16)
    attended = jnp.dot(prob_low, head_value, preferred_element_type=jnp.float32).astype(
        jnp.bfloat16
    )
    row_delta = jnp.sum(
        head_grad.astype(jnp.float32) * attended.astype(jnp.float32), axis=1, keepdims=True
    )
    grad_prob = lax.dot_general(
        head_grad, head_value, (((1,), (1,)), ((), ())), preferred_element_type=jnp.float32
    )
    grad_score = (softmax * (grad_prob - row_delta) * scaling).astype(jnp.bfloat16)
    grad_q = jnp.dot(grad_score, head_key, preferred_element_type=jnp.float32).astype(jnp.bfloat16)
    grad_k = lax.dot_general(
        grad_score, head_query, (((0,), (0,)), ((), ())), preferred_element_type=jnp.float32
    )
    grad_v = lax.dot_general(
        prob_low, head_grad, (((0,), (0,)), ((), ())), preferred_element_type=jnp.float32
    )
    return (attended, grad_q, grad_k, grad_v)


def split_heads(matrix, width):
    return matrix.reshape(matrix.shape[0], -1, width).transpose(1, 0, 2)


def merge_heads(stacked):
    return stacked.transpose(1, 0, 2).reshape(stacked.shape[1], -1)


def per_device(image_query, image_key, image_value, text_key, text_value, out_weight, cotangent):
    queries = image_query[0]
    own_keys = image_key[0]
    own_values = image_value[0]
    grad_out = cotangent[0]
    tokens = queries.shape[0]
    earlier = []
    moving = (own_keys, own_values)
    for distance in range(1, STEPS):
        moving = from_behind((moving[0], moving[1]), "seq", 1)
        earlier.append(moving)
    full_weight = lax.all_gather(out_weight, "fsdp", axis=0, tiled=True)
    grad_attended = lax.dot_general(
        grad_out, full_weight, (((1,), (1,)), ((), ())), preferred_element_type=jnp.float32
    ).astype(jnp.bfloat16)
    ordered = [earlier[distance - 1] for distance in range(STEPS - 1, 0, -1)]
    set_keys = jnp.concatenate(
        [text_key[0]] + [member[0] for member in ordered] + [own_keys], axis=0
    )
    set_values = jnp.concatenate(
        [text_value[0]] + [member[1] for member in ordered] + [own_values], axis=0
    )
    attended, grad_q, grad_k, grad_v = lax.map(
        head_pass,
        (
            split_heads(queries, HEAD_DIM),
            split_heads(set_keys, HEAD_DIM),
            split_heads(set_values, HEAD_DIM),
            split_heads(grad_attended, HEAD_DIM),
        ),
    )
    attended = merge_heads(attended)
    grad_q = merge_heads(grad_q)
    grad_k = merge_heads(grad_k)
    grad_v = merge_heads(grad_v)
    text_rows = text_key.shape[1]

    def block_part(distance):
        first_row = text_rows + (STEPS - 1 - distance) * tokens
        return (grad_k[first_row : first_row + tokens], grad_v[first_row : first_row + tokens])

    carried = block_part(STEPS - 1)
    for distance in range(STEPS - 2, -1, -1):
        carried = from_behind((carried[0], carried[1]), "seq", -1)
        own_part = block_part(distance)
        carried = (carried[0] + own_part[0], carried[1] + own_part[1])
    image_out = jnp.dot(attended, full_weight, preferred_element_type=jnp.float32).astype(
        jnp.bfloat16
    )
    weight_terms = lax.dot_general(
        attended, grad_out, (((0,), (0,)), ((), ())), preferred_element_type=jnp.float32
    )
    weight_rows = lax.psum_scatter(
        weight_terms.astype(jnp.bfloat16), "fsdp", scatter_dimension=0, tiled=True
    ).astype(jnp.float32)
    grad_weight = lax.psum_scatter(weight_rows, "seq", scatter_dimension=0, tiled=True)
    return (
        image_out[None],
        grad_q[None],
        carried[0].astype(jnp.bfloat16)[None],
        carried[1].astype(jnp.bfloat16)[None],
        grad_weight,
    )


def solution(mesh):
    in_specs = (
        P("fsdp", "seq", None),
        P("fsdp", "seq", None),
        P("fsdp", "seq", None),
        P("fsdp", None, None),
        P("fsdp", None, None),
        P("fsdp", None),
        P("fsdp", "seq", None),
    )
    out_specs = (
        P("fsdp", "seq", None),
        P("fsdp", "seq", None),
        P("fsdp", "seq", None),
        P("fsdp", "seq", None),
        P(("fsdp", "seq"), None),
    )
    return jax.shard_map(
        per_device, mesh=mesh, in_specs=in_specs, out_specs=out_specs, check_vma=False
    )
```

profile of v0, /device:TPU:2, one launch (start us, length us, event | category | flops | bytes accessed | tf_op | source)
XLA Modules:
  0.0 815.3 jit_solution(9046898829631140023)
XLA Ops:
  11.8 17.7 %collective-permute-done = bf16[256,1536]{0,1:T(8,128)(2,1)} collective-permute-done((bf16[256,1536]{0,1:T(8,128)(2,1)S(1)}, bf16[256,1536]{0,1:T(8,128)(2,1)}, u32[]{:S(2)}, u32[]{:S(2)}) %collective-permute-start) | collective-permute-done | bytes 786464 | tf_op jit(solution)/shard_map/ppermute | solution.py:15
  30.8 15.6 %collective-permute-done.3 = bf16[256,1536]{0,1:T(8,128)(2,1)} collective-permute-done((bf16[256,1536]{0,1:T(8,128)(2,1)S(1)}, bf16[256,1536]{0,1:T(8,128)(2,1)}, u32[]{:S(2)}, u32[]{:S(2)}) %collective-permute-start.3) | collective-permute-done | bytes 786464 | tf_op jit(solution)/shard_map/ppermute | solution.py:15
  47.6 15.6 %collective-permute-done.1 = bf16[256,1536]{0,1:T(8,128)(2,1)} collective-permute-done((bf16[256,1536]{0,1:T(8,128)(2,1)}, bf16[256,1536]{0,1:T(8,128)(2,1)}, u32[]{:S(2)}, u32[]{:S(2)}) %collective-permute-start.1) | collective-permute-done | bytes 786464 | tf_op jit(solution)/shard_map/ppermute | solution.py:15
  64.5 2.7 copy.42
  68.9 2.3 copy.41
  71.1 8.9 %collective-permute-done.4 = bf16[256,1536]{0,1:T(8,128)(2,1)} collective-permute-done((bf16[256,1536]{0,1:T(8,128)(2,1)}, bf16[256,1536]{0,1:T(8,128)(2,1)}, u32[]{:S(2)}, u32[]{:S(2)}) %collective-permute-start.4) | collective-permute-done | bytes 786464 | tf_op jit(solution)/shard_map/ppermute | solution.py:15
  81.3 2.7 constant_dynamic-update-slice_fusion.5
  85.4 11.5 %collective-permute-done.2 = bf16[256,1536]{0,1:T(8,128)(2,1)} collective-permute-done((bf16[256,1536]{0,1:T(8,128)(2,1)}, bf16[256,1536]{0,1:T(8,128)(2,1)}, u32[]{:S(2)}, u32[]{:S(2)}) %collective-permute-start.2) | collective-permute-done | bytes 786464 | tf_op jit(solution)/shard_map/ppermute | solution.py:15
  96.9 2.2 constant_dynamic-update-slice_fusion.4
  99.1 2.2 constant_dynamic-update-slice_fusion.3
  101.3 2.1 constant_dynamic-update-slice_fusion.2
  104.5 7.8 collective-permute-done.5
  113.3 2.3 constant_dynamic-update-slice_fusion.8
  115.6 2.2 constant_dynamic-update-slice_fusion.7
  118.8 3.7 convolution_convert_fusion.4
  123.7 126.2 %while.16 = (s32[]{:T(128)}, bf16[12,256,128]{1,2,0:T(8,128)(2,1)S(1)}, bf16[12,256,128]{1,2,0:T(8,128)(2,1)}, f32[12,1536,128]{1,2,0:T(8,128)}, f32[12,1536,128...) while((s32[]{:T(128)}, ...), condition=%wide.region_4.5_spmd, body=%wide.region_0.4_spmd.sunk | while | flops 610467072 | bytes 14238825 | solution.py:81
  130.1 2.0 fusion.75
  140.6 2.0 fusion.75
  151.1 2.0 fusion.75
  161.6 2.0 fusion.75
  172.1 2.0 fusion.75
  182.6 2.0 fusion.75
  193.1 2.1 fusion.75
  203.7 2.0 fusion.75
  214.2 2.0 fusion.75
  224.7 2.1 fusion.75
  235.2 2.1 fusion.75
  245.8 2.0 fusion.75
  250.0 3.5 convolution_convert_fusion.2
  253.5 5.0 fusion.41
  258.5 39.4 %collective-permute-start.9 = (f32[256,1536]{0,1:T(8,128)S(1)}, f32[256,1536]{0,1:T(8,128)S(1)}, u32[]{:S(2)}, u32[]{:S(2)}) collective-permute-start(f32[256,1536]{0,1:T(8,128)S(1)} %bitcast.156), channel_id=1, source_target_pairs={{4,0},{8,4},{12,8},{16,12},{20,16},{24,20},{28,24},{32,28},{36,32}... | collective-permute-start | bytes 4718600 | tf_op jit(solution)/shard_map/ppermute | solution.py:15
  301.6 31.1 %collective-permute-done.9 = f32[256,1536]{0,1:T(8,128)S(1)} collective-permute-done((f32[256,1536]{0,1:T(8,128)S(1)}, f32[256,1536]{0,1:T(8,128)S(1)}, u32[]{:S(2)}, u32[]{:S(2)}) %collective-permute-start.9) | collective-permute-done | bytes 1572896 | tf_op jit(solution)/shard_map/ppermute | solution.py:15
  332.9 2.6 collective-permute-start.10
  335.5 30.9 %collective-permute-done.6 = f32[256,1536]{0,1:T(8,128)S(1)} collective-permute-done((f32[256,1536]{0,1:T(8,128)S(1)}, f32[256,1536]{0,1:T(8,128)S(1)}, u32[]{:S(2)}, u32[]{:S(2)}) %collective-permute-start.6) | collective-permute-done | bytes 1572896 | tf_op jit(solution)/shard_map/ppermute | solution.py:15
  366.6 2.6 collective-permute-start.7
  369.2 30.9 %collective-permute-done.10 = f32[256,1536]{0,1:T(8,128)S(1)} collective-permute-done((f32[256,1536]{0,1:T(8,128)S(1)}, f32[256,1536]{0,1:T(8,128)S(1)}, u32[]{:S(2)}, u32[]{:S(2)}) %collective-permute-start.10) | collective-permute-done | bytes 1572896 | tf_op jit(solution)/shard_map/ppermute | solution.py:15
  401.5 2.5 collective-permute-start.11
  404.0 29.8 %collective-permute-done.7 = f32[256,1536]{0,1:T(8,128)S(1)} collective-permute-done((f32[256,1536]{0,1:T(8,128)S(1)}, f32[256,1536]{0,1:T(8,128)S(1)}, u32[]{:S(2)}, u32[]{:S(2)}) %collective-permute-start.7) | collective-permute-done | bytes 1572896 | tf_op jit(solution)/shard_map/ppermute | solution.py:15
  435.2 2.5 collective-permute-start.8
  439.3 297.7 %fusion = f32[8,1536]{1,0:T(8,128)S(1)} fusion(f32[384,1536]{1,0:T(8,128)S(1)} %convert_element_type.41), kind=kCustom, calls=%all-reduce-scatter | all-reduce-scatter fusion | flops 786433 | bytes 2409472
  739.5 4.3 collective-permute-start.12
  747.8 20.7 %collective-permute-start.16 = (f32[8,1536]{1,0:T(8,128)S(1)}, f32[8,1536]{1,0:T(8,128)S(1)}, u32[]{:S(2)}, u32[]{:S(2)}) collective-permute-start(f32[8,1536]{1,0:T(8,128)S(1)} %fusion), channel_id=1, source_target_pairs={{0,20},{4,24},{8,28},{12,32},{16,36},{20,40},{24,44},{28,48},{32,5... | collective-permute-start | bytes 147464
  768.5 4.9 fusion.35
  774.5 2.6 collective-permute-start.17
  778.4 3.9 collective-permute-start.19
  784.4 5.7 collective-permute-start.21
  793.4 2.2 collective-permute-start.23
  795.7 2.3 collective-permute-start.24
  (215 shorter events, 150.8 us)
Async XLA Ops:
  7.2 111.7 %copy-start = (bf16[1,256,1536]{2,1,0:T(8,128)(2,1)S(1)}, bf16[1,256,1536]{2,1,0:T(8,128)(2,1)}, u32[]{:S(2)}) copy-start(bf16[1,256,1536]{2,1,0:T(8,128)(2,1)} %param.15) | copy-start | bytes 2359300
  7.2 3.1 copy-start.9
  7.2 111.6 %all-gather.2.cloned.1.call-start = ((), (), s32[]{:S(2)}) async-start(), calls=%async_computation.1 | async-start | bytes 5898240 | tf_op jit(solution)/shard_map/all_gather | solution.py:70
  7.9 429.7 %reduce-scatter.4.cloned.1.call-start = ((), (), s32[]{:S(2)}) async-start(), calls=%async_computation.2 | async-start | bytes 5898240 | tf_op jit(solution)/shard_map/reduce_scatter | solution.py:111
  8.7 55.8 %copy-start.4 = (bf16[1,256,1536]{1,2,0:T(8,128)(2,1)}, bf16[1,256,1536]{1,2,0:T(8,128)(2,1)S(1)}, u32[]{:S(2)}) copy-start(bf16[1,256,1536]{1,2,0:T(8,128)(2,1)S(1)} %copy.43) | copy-start | bytes 2359300
  8.7 20.8 %collective-permute-start = (bf16[256,1536]{0,1:T(8,128)(2,1)S(1)}, bf16[256,1536]{0,1:T(8,128)(2,1)}, u32[]{:S(2)}, u32[]{:S(2)}) collective-permute-start(bf16[256,1536]{0,1:T(8,128)(2,1)S(1)} %bitcast.147), channel_id=1, source_target_pairs={{252,0},{0,4},{4,8},{8,12},{12,16},{16,20},{20,24},{24,28},{28,32}... | collective-permute-start | bytes 2359304 | tf_op jit(solution)/shard_map/ppermute | solution.py:15
  10.5 35.8 %collective-permute-start.3 = (bf16[256,1536]{0,1:T(8,128)(2,1)S(1)}, bf16[256,1536]{0,1:T(8,128)(2,1)}, u32[]{:S(2)}, u32[]{:S(2)}) collective-permute-start(bf16[256,1536]{0,1:T(8,128)(2,1)S(1)} %bitcast.145), channel_id=1, source_target_pairs={{252,0},{0,4},{4,8},{8,12},{12,16},{16,20},{20,24},{24,28},{28,32}... | collective-permute-start | bytes 2359304 | tf_op jit(solution)/shard_map/ppermute | solution.py:15
  29.5 33.7 %collective-permute-start.1 = (bf16[256,1536]{0,1:T(8,128)(2,1)}, bf16[256,1536]{0,1:T(8,128)(2,1)}, u32[]{:S(2)}, u32[]{:S(2)}) collective-permute-start(bf16[256,1536]{0,1:T(8,128)(2,1)} %collective-permute-done), channel_id=1, source_target_pairs={{252,0},{0,4},{4,8},{8,12},{12,16},{16,20},{20,24},{24,28},{28,32}... | collective-permute-start | bytes 2359304 | tf_op jit(solution)/shard_map/ppermute | solution.py:15
  46.3 33.7 %collective-permute-start.4 = (bf16[256,1536]{0,1:T(8,128)(2,1)}, bf16[256,1536]{0,1:T(8,128)(2,1)}, u32[]{:S(2)}, u32[]{:S(2)}) collective-permute-start(bf16[256,1536]{0,1:T(8,128)(2,1)} %collective-permute-done.3), channel_id=1, source_target_pairs={{252,0},{0,4},{4,8},{8,12},{12,16},{16,20},{20,24},{24,28},{28,32}... | collective-permute-start | bytes 2359304 | tf_op jit(solution)/shard_map/ppermute | solution.py:15
  63.2 33.7 %collective-permute-start.2 = (bf16[256,1536]{0,1:T(8,128)(2,1)}, bf16[256,1536]{0,1:T(8,128)(2,1)}, u32[]{:S(2)}, u32[]{:S(2)}) collective-permute-start(bf16[256,1536]{0,1:T(8,128)(2,1)} %collective-permute-done.1), channel_id=1, source_target_pairs={{252,0},{0,4},{4,8},{8,12},{12,16},{16,20},{20,24},{24,28},{28,32}... | collective-permute-start | bytes 2359304 | tf_op jit(solution)/shard_map/ppermute | solution.py:15
  80.1 32.2 %collective-permute-start.5 = (bf16[256,1536]{0,1:T(8,128)(2,1)}, bf16[256,1536]{0,1:T(8,128)(2,1)S(1)}, u32[]{:S(2)}, u32[]{:S(2)}) collective-permute-start(bf16[256,1536]{0,1:T(8,128)(2,1)} %collective-permute-done.4), channel_id=1, source_target_pairs={{252,0},{0,4},{4,8},{8,12},{12,16},{16,20},{20,24},{24,28},{28,32}... | collective-permute-start | bytes 2359304 | tf_op jit(solution)/shard_map/ppermute | solution.py:15
  99.1 4.3 copy-start.5
  250.0 3.5 copy-start.7
  253.5 44.4 %copy-start.3 = (f32[12,1536,128]{1,2,0:T(8,128)S(1)}, f32[12,1536,128]{1,2,0:T(8,128)}, u32[]{:S(2)}) copy-start(f32[12,1536,128]{1,2,0:T(8,128)} %get-tuple-element.57) | copy-start | bytes 28311556
  258.5 74.2 %collective-permute-start.9 = (f32[256,1536]{0,1:T(8,128)S(1)}, f32[256,1536]{0,1:T(8,128)S(1)}, u32[]{:S(2)}, u32[]{:S(2)}) collective-permute-start(f32[256,1536]{0,1:T(8,128)S(1)} %bitcast.156), channel_id=1, source_target_pairs={{4,0},{8,4},{12,8},{16,12},{20,16},{24,20},{28,24},{32,28},{36,32}... | collective-permute-start | bytes 4718600 | tf_op jit(solution)/shard_map/ppermute | solution.py:15
  299.8 66.6 %collective-permute-start.6 = (f32[256,1536]{0,1:T(8,128)S(1)}, f32[256,1536]{0,1:T(8,128)S(1)}, u32[]{:S(2)}, u32[]{:S(2)}) collective-permute-start(f32[256,1536]{0,1:T(8,128)S(1)} %bitcast.155), channel_id=1, source_target_pairs={{4,0},{8,4},{12,8},{16,12},{20,16},{24,20},{28,24},{32,28},{36,32}... | collective-permute-start | bytes 4718600 | tf_op jit(solution)/shard_map/ppermute | solution.py:15
  332.9 67.2 %collective-permute-start.10 = (f32[256,1536]{0,1:T(8,128)S(1)}, f32[256,1536]{0,1:T(8,128)S(1)}, u32[]{:S(2)}, u32[]{:S(2)}) collective-permute-start(f32[256,1536]{0,1:T(8,128)S(1)} %bitcast_add_fusion.2), channel_id=1, source_target_pairs={{4,0},{8,4},{12,8},{16,12},{20,16},{24,20},{28,24},{32,28},{36,32}... | collective-permute-start | bytes 4718600 | tf_op jit(solution)/shard_map/ppermute | solution.py:15
  366.6 67.2 %collective-permute-start.7 = (f32[256,1536]{0,1:T(8,128)S(1)}, f32[256,1536]{0,1:T(8,128)S(1)}, u32[]{:S(2)}, u32[]{:S(2)}) collective-permute-start(f32[256,1536]{0,1:T(8,128)S(1)} %bitcast_add_fusion.5), channel_id=1, source_target_pairs={{4,0},{8,4},{12,8},{16,12},{20,16},{24,20},{28,24},{32,28},{36,32}... | collective-permute-start | bytes 4718600 | tf_op jit(solution)/shard_map/ppermute | solution.py:15
  401.5 343.6 %collective-permute-start.11 = (f32[256,1536]{0,1:T(8,128)}, f32[256,1536]{0,1:T(8,128)}, u32[]{:S(2)}, u32[]{:S(2)}) collective-permute-start(f32[256,1536]{0,1:T(8,128)} %bitcast_add_fusion.1), channel_id=1, source_target_pairs={{4,0},{8,4},{12,8},{16,12},{20,16},{24,20},{28,24},{32,28},{36,32}... | collective-permute-start | bytes 4718600 | tf_op jit(solution)/shard_map/ppermute | solution.py:15
  435.2 311.2 %collective-permute-start.8 = (f32[256,1536]{0,1:T(8,128)}, f32[256,1536]{0,1:T(8,128)}, u32[]{:S(2)}, u32[]{:S(2)}) collective-permute-start(f32[256,1536]{0,1:T(8,128)} %bitcast_add_fusion.4), channel_id=1, source_target_pairs={{4,0},{8,4},{12,8},{16,12},{20,16},{24,20},{28,24},{32,28},{36,32}... | collective-permute-start | bytes 4718600 | tf_op jit(solution)/shard_map/ppermute | solution.py:15
  439.2 299.0 %copy-start.19 = (u32[256]{0:T(256)S(1)}, u32[256]{0:T(256)}, u32[]{:S(2)}) copy-start(u32[256]{0:T(256)} %constant.37) | copy-start | bytes 3076
  737.0 10.8 %collective-permute-start.27 = (f32[6,1536]{1,0:T(8,128)S(1)}, f32[6,1536]{1,0:T(8,128)S(1)}, u32[]{:S(2)}, u32[]{:S(2)}) collective-permute-start(f32[6,1536]{1,0:T(8,128)S(1)} %slice.72), channel_id=1, source_target_pairs={{0,64},{4,68},{8,72},{12,76},{16,80},{20,84},{24,88},{28,92},{32,9... | collective-permute-start | bytes 110600
  739.5 33.9 %copy-start.10 = (bf16[12,256,128]{1,2,0:T(8,128)(2,1)S(1)}, bf16[12,256,128]{1,2,0:T(8,128)(2,1)}, u32[]{:S(2)}) copy-start(bf16[12,256,128]{1,2,0:T(8,128)(2,1)} %get-tuple-element.56) | copy-start | bytes 2359300
  739.5 35.0 %collective-permute-start.12 = (f32[8,1536]{1,0:T(8,128)S(1)}, f32[8,1536]{1,0:T(8,128)S(1)}, u32[]{:S(2)}, u32[]{:S(2)}) collective-permute-start(f32[8,1536]{1,0:T(8,128)S(1)} %fusion), channel_id=1, source_target_pairs={{0,4},{4,8},{8,12},{12,16},{16,20},{20,24},{24,28},{28,32},{32,36}... | collective-permute-start | bytes 147464
  743.8 33.3 %collective-permute-start.13 = (f32[8,1536]{1,0:T(8,128)S(1)}, f32[8,1536]{1,0:T(8,128)S(1)}, u32[]{:S(2)}, u32[]{:S(2)}) collective-permute-start(f32[8,1536]{1,0:T(8,128)S(1)} %fusion), channel_id=1, source_target_pairs={{0,8},{4,12},{8,16},{12,20},{16,24},{20,28},{24,32},{28,36},{32,40... | collective-permute-start | bytes 147464
  745.1 33.3 %collective-permute-start.14 = (f32[8,1536]{1,0:T(8,128)S(1)}, f32[8,1536]{1,0:T(8,128)S(1)}, u32[]{:S(2)}, u32[]{:S(2)}) collective-permute-start(f32[8,1536]{1,0:T(8,128)S(1)} %fusion), channel_id=1, source_target_pairs={{0,12},{4,16},{8,20},{12,24},{16,28},{20,32},{24,36},{28,40},{32,4... | collective-permute-start | bytes 147464
  746.5 36.0 %collective-permute-start.15 = (f32[8,1536]{1,0:T(8,128)S(1)}, f32[8,1536]{1,0:T(8,128)S(1)}, u32[]{:S(2)}, u32[]{:S(2)}) collective-permute-start(f32[8,1536]{1,0:T(8,128)S(1)} %fusion), channel_id=1, source_target_pairs={{0,16},{4,20},{8,24},{12,28},{16,32},{20,36},{24,40},{28,44},{32,4... | collective-permute-start | bytes 147464
  747.8 36.6 %collective-permute-start.16 = (f32[8,1536]{1,0:T(8,128)S(1)}, f32[8,1536]{1,0:T(8,128)S(1)}, u32[]{:S(2)}, u32[]{:S(2)}) collective-permute-start(f32[8,1536]{1,0:T(8,128)S(1)} %fusion), channel_id=1, source_target_pairs={{0,20},{4,24},{8,28},{12,32},{16,36},{20,40},{24,44},{28,48},{32,5... | collective-permute-start | bytes 147464
  773.4 16.7 %copy-start.2 = (f32[256,12,128]{0,2,1:T(8,128)S(1)}, f32[256,12,128]{0,2,1:T(8,128)}, u32[]{:S(2)}) copy-start(f32[256,12,128]{0,2,1:T(8,128)} %get-tuple-element.118) | copy-start | bytes 4718596
  774.5 17.3 %collective-permute-start.17 = (f32[8,1536]{1,0:T(8,128)S(1)}, f32[8,1536]{1,0:T(8,128)S(1)}, u32[]{:S(2)}, u32[]{:S(2)}) collective-permute-start(f32[8,1536]{1,0:T(8,128)S(1)} %fusion), channel_id=1, source_target_pairs={{0,24},{4,28},{8,32},{12,36},{16,40},{20,44},{24,48},{28,52},{32,5... | collective-permute-start | bytes 147464
  777.1 16.3 %collective-permute-start.18 = (f32[8,1536]{1,0:T(8,128)S(1)}, f32[8,1536]{1,0:T(8,128)S(1)}, u32[]{:S(2)}, u32[]{:S(2)}) collective-permute-start(f32[8,1536]{1,0:T(8,128)S(1)} %fusion), channel_id=1, source_target_pairs={{0,28},{4,32},{8,36},{12,40},{16,44},{20,48},{24,52},{28,56},{32,6... | collective-permute-start | bytes 147464
  778.4 17.2 %collective-permute-start.19 = (f32[8,1536]{1,0:T(8,128)S(1)}, f32[8,1536]{1,0:T(8,128)S(1)}, u32[]{:S(2)}, u32[]{:S(2)}) collective-permute-start(f32[8,1536]{1,0:T(8,128)S(1)} %fusion), channel_id=1, source_target_pairs={{0,32},{4,36},{8,40},{12,44},{16,48},{20,52},{24,56},{28,60},{32,6... | collective-permute-start | bytes 147464
  782.4 15.6 %collective-permute-start.20 = (f32[8,1536]{1,0:T(8,128)S(1)}, f32[8,1536]{1,0:T(8,128)S(1)}, u32[]{:S(2)}, u32[]{:S(2)}) collective-permute-start(f32[8,1536]{1,0:T(8,128)S(1)} %fusion), channel_id=1, source_target_pairs={{0,36},{4,40},{8,44},{12,48},{16,52},{20,56},{24,60},{28,64},{32,6... | collective-permute-start | bytes 147464
  784.4 15.5 %collective-permute-start.21 = (f32[8,1536]{1,0:T(8,128)S(1)}, f32[8,1536]{1,0:T(8,128)S(1)}, u32[]{:S(2)}, u32[]{:S(2)}) collective-permute-start(f32[8,1536]{1,0:T(8,128)S(1)} %fusion), channel_id=1, source_target_pairs={{0,40},{4,44},{8,48},{12,52},{16,56},{20,60},{24,64},{28,68},{32,7... | collective-permute-start | bytes 147464
  790.1 11.8 %copy-start.1 = (f32[256,12,128]{0,2,1:T(8,128)S(1)}, f32[256,12,128]{0,2,1:T(8,128)}, u32[]{:S(2)}) copy-start(f32[256,12,128]{0,2,1:T(8,128)} %get-tuple-element.122) | copy-start | bytes 4718596
  791.9 14.0 %collective-permute-start.22 = (f32[8,1536]{1,0:T(8,128)S(1)}, f32[8,1536]{1,0:T(8,128)S(1)}, u32[]{:S(2)}, u32[]{:S(2)}) collective-permute-start(f32[8,1536]{1,0:T(8,128)S(1)} %fusion), channel_id=1, source_target_pairs={{0,44},{4,48},{8,52},{12,56},{16,60},{20,64},{24,68},{28,72},{32,7... | collective-permute-start | bytes 147464
  793.4 10.1 %copy-start.11 = (f32[8,1536]{1,0:T(8,128)}, f32[8,1536]{1,0:T(8,128)S(1)}, u32[]{:S(2)}) copy-start(f32[8,1536]{1,0:T(8,128)S(1)} %collective-permute-done.18) | copy-start | bytes 147460
  793.4 12.5 %collective-permute-start.23 = (f32[8,1536]{1,0:T(8,128)S(1)}, f32[8,1536]{1,0:T(8,128)S(1)}, u32[]{:S(2)}, u32[]{:S(2)}) collective-permute-start(f32[8,1536]{1,0:T(8,128)S(1)} %fusion), channel_id=1, source_target_pairs={{0,48},{4,52},{8,56},{12,60},{16,64},{20,68},{24,72},{28,76},{32,8... | collective-permute-start | bytes 147464
  795.7 7.8 copy-start.13
  795.7 10.2 %collective-permute-start.24 = (f32[8,1536]{1,0:T(8,128)S(1)}, f32[8,1536]{1,0:T(8,128)S(1)}, u32[]{:S(2)}, u32[]{:S(2)}) collective-permute-start(f32[8,1536]{1,0:T(8,128)S(1)} %fusion), channel_id=1, source_target_pairs={{0,52},{4,56},{8,60},{12,64},{16,68},{20,72},{24,76},{28,80},{32,8... | collective-permute-start | bytes 147464
  798.0 5.5 copy-start.15
  798.0 7.9 collective-permute-start.25
  799.9 3.6 copy-start.17
  799.9 6.0 collective-permute-start.26
  803.5 2.4 copy-start.12
  803.6 2.4 copy-start.14
  803.6 2.4 copy-start.16
  803.6 2.4 copy-start.18
  (2 other events, 2.3 us)
Sparse Core Ops, SparseCore 0:
  9.8 55.5 all-gather.1
  253.6 84.5 reduce-scatter.3
where the time goes:
time: 819 us; the launch traced here: 815 us
  blocking collectives  298 us (36%)
  waiting for transfers between devices  201 us (25%)
  matrix products  124 us (15%)
  starting transfers between devices  115 us (14%)
  local copies, waits for them, and re-layouts  49.5 us (6%)
  between operations  15.3 us (2%)
  other arithmetic  13.1 us (2%)
    unnamed x1, blocking collectives  298 us
    ppermute x12, waiting for transfers between devices, from_behind(): return lax.ppermute(block, axis, route)  200 us
    ppermute x12, starting transfers between devices, from_behind(): return lax.ppermute(block, axis, route)  59.2 us
    unnamed x16, starting transfers between devices  55.6 us
    unnamed x60, local copies, waits for them, and re-layouts  31.3 us
    dot_general x12, matrix products, head_pass(): lax.dot_general(grad_score, head_query, (((0,), (0,)), ((), ())), preferr...  24.2 us
    dot_general x12, matrix products, head_pass(): lax.dot_general(head_grad, head_value, (((1,), (1,)), ((), ())), preferre...  18.5 us
    dot_general x12, matrix products, head_pass(): jnp.dot(prob_low, head_value, preferred_element_type=jnp.float32)  18 us
  transfers between devices with their start and end apart: 30, of which 10 were waited for; matrix products, arithmetic and copies ran while one was open for 43% of the time, Pallas kernels for 0%

commit v1 on v0

v1 whole, which is shorter than its diff:
```python
import functools
import math

import jax
import jax.numpy as jnp
from jax import lax
from jax.experimental import pallas as pl
from jax.experimental.pallas import tpu as pltpu
from jax.sharding import PartitionSpec as P

F32 = jnp.float32
BF16 = jnp.bfloat16
MESH = pl.DeviceIdType.MESH
HEAD = 128
TOK = 256
TEXT = 512
INNER = 1536
SCALE = 1.0 / math.sqrt(HEAD)
COEF = SCALE * math.log2(math.e)
HALO = 3 * TOK
OWN = TEXT + HALO
KEYS = OWN + 4 * TOK
SHARD = 384


def dot(a, b, ca, cb):
    return lax.dot_general(a, b, (((ca,), (cb,)), ((), ())), preferred_element_type=F32)


def rows_at(start, size):
    return pl.ds(pl.multiple_of(start, size), size)


def forward_unit(query, key_at, value_at, prob_ref, score_ref):
    peak = None
    for i in range(6):
        score = dot(key_at(i), query, 1, 1)
        score_ref[i] = score
        part = jnp.max(score, axis=0, keepdims=True)
        peak = part if peak is None else jnp.maximum(peak, part)
    peak = peak * COEF
    total = None
    attended = None
    for i in range(6):
        prob = jnp.exp2(score_ref[i] * COEF - peak)
        part = jnp.sum(prob, axis=0, keepdims=True)
        total = part if total is None else total + part
        low = prob.astype(BF16)
        prob_ref[i] = low
        term = dot(value_at(i), low, 0, 0)
        attended = term if attended is None else attended + term
    inverse = 1.0 / total
    return (attended * inverse).T.astype(BF16), inverse


def backward_unit(query, grad, attended, inverse, key_at, value_at, prob_ref, add_key, add_value):
    grad32 = grad.astype(F32)
    delta = jnp.sum((grad32 * attended.astype(F32)).T, axis=0, keepdims=True)
    query_t = (query.astype(F32).T * (inverse * SCALE)).astype(BF16)
    grad_t = (grad32.T * inverse).astype(BF16)
    total = None
    for i in range(6):
        grad_prob = dot(value_at(i), grad, 1, 1)
        low = prob_ref[i]
        grad_score = (low.astype(F32) * (grad_prob - delta)).astype(BF16)
        term = dot(key_at(i), grad_score, 0, 0)
        total = term if total is None else total + term
        if i >= 2:
            add_key(i - 2, dot(grad_score, query_t, 1, 1))
            add_value(i - 2, dot(low, grad_t, 1, 1))
    return (total * (inverse * SCALE)).T.astype(BF16)


def device(x, y, z, core):
    return ((y // 2) * 32 + z * 4 + x, (y % 2) * 2 + core)


def kernel(
    q_hbm, k_hbm, v_hbm, tk_hbm, tv_hbm, w_hbm, cot_hbm,
    img_hbm, dq_hbm, dk_hbm, dv_hbm, gw_ref,
    img, cot, wf, kb, vb, qb, gs, gb, prob, score, stat, ob, dqb, att,
    dka, dva, hsk, hsv, hrk, hrv, okb, ovb,
    relf, relb, gacc, gsend, grecv, ysend, yrecv, gsum, hsend, hrecv, yown, zsend, zrecv, xsend, xrecv,
    lsem, s_in, r_in, s_gr, r_gr, s_w, r_w, s_halo, r_halo,
    r_rf, s_rf, r_rb, s_rb, s_att, r_att, s_dq, r_dq, s_dkv, r_dkv, s_hb, r_hb,
    s_c, r_c, s_y, r_y, s_h, r_h, s_z, r_z, s_x, r_x,
):
    seq = lax.axis_index("seq")
    fsdp = lax.axis_index("fsdp")
    x = lax.rem(seq, 4)
    z = lax.rem(seq // 4, 8)
    yh = seq // 32
    yl = fsdp // 2
    y = yh * 2 + yl
    core = lax.rem(fsdp, 2)
    zz = yh * 8 + z

    def x_peer(d):
        return device(lax.rem(x + d, 4), y, z, core)

    def y_peer(d):
        return device(x, lax.rem(y + d, 4), z, core)

    def z_peer(d):
        return device(x, y, lax.rem(z + d, 8), core)

    def other_core():
        return device(x, y, z, 1 - core)

    def super_peer(d):
        there = lax.rem(zz + d, 16)
        return device(x, (there // 8) * 2 + yl, lax.rem(there, 8), core)

    def remote(src, dst, ssem, rsem, dev):
        return pltpu.make_async_remote_copy(
            src_ref=src, dst_ref=dst, send_sem=ssem, recv_sem=rsem,
            device_id=dev, device_id_type=MESH,
        )

    pending = []

    def send(*args):
        copy = remote(*args)
        copy.start()
        pending.append(copy)

    def got(dst, ssem, rsem):
        remote(dst, dst, ssem, rsem, other_core()).wait_recv()

    barrier = pltpu.get_barrier_semaphore()
    peers = [x_peer(d) for d in (1, 2, 3)] + [y_peer(d) for d in (1, 2, 3)]
    peers += [z_peer(d) for d in range(1, 8)] + [other_core(), super_peer(1), super_peer(15)]
    for peer in peers:
        pl.semaphore_signal(barrier, inc=1, device_id=peer, device_id_type=MESH)

    locals_ = {}
    count = [0]

    def local(name, src, dst):
        copy = pltpu.make_async_copy(src, dst, lsem.at[count[0]])
        count[0] += 1
        copy.start()
        locals_[name] = copy

    def head(owner, c):
        return rows_at((owner * 3 + c) * HEAD, HEAD)

    own_rows = rows_at(OWN + x * TOK, TOK)
    q_rows = rows_at(x * TOK, TOK)
    local("cot", cot_hbm, cot)
    local("w", w_hbm, wf.at[rows_at(fsdp * SHARD, SHARD)])
    for c in range(3):
        local(("k", c), k_hbm.at[:, head(x, c)], kb.at[c, own_rows])
        local(("v", c), v_hbm.at[:, head(x, c)], vb.at[c, own_rows])
        local(("q", c), q_hbm.at[:, head(x, c)], qb.at[c, q_rows])
        local(("tk", c), tk_hbm.at[:, head(x, c)], kb.at[c, 0:TEXT])
        local(("tv", c), tv_hbm.at[:, head(x, c)], vb.at[c, 0:TEXT])
    for c in range(3):
        dka[c] = jnp.zeros((7 * TOK, HEAD), F32)
        dva[c] = jnp.zeros((7 * TOK, HEAD), F32)
    pl.semaphore_wait(barrier, len(peers))

    half = SHARD // 2
    for d, part in ((1, 0), (3, 1)):
        send(w_hbm.at[part * half:(part + 1) * half], wf.at[rows_at(fsdp * SHARD + part * half, half)],
             s_w.at[part], r_w.at[part], y_peer(d))
    send(w_hbm, wf.at[rows_at(fsdp * SHARD, SHARD)], s_w.at[2], r_w.at[2], other_core())

    for c in range(3):
        for t, (src, dst, at) in enumerate(((k_hbm, kb, own_rows), (v_hbm, vb, own_rows), (q_hbm, qb, q_rows))):
            for d in (1, 3, 2):
                send(src.at[:, head(lax.rem(x + d, 4), c)], dst.at[c, at],
                     s_in.at[t, c, d - 1], r_in.at[t, c, d - 1], x_peer(d))
    def got_in(t, c):
        dst, base = ((kb, OWN), (vb, OWN), (qb, 0))[t]
        for d in (1, 2, 3):
            got(dst.at[c, rows_at(base + lax.rem(x + 4 - d, 4) * TOK, TOK)],
                s_in.at[t, c, d - 1], r_in.at[t, c, d - 1])
        locals_[("k", c) if t == 0 else ("v", c) if t == 1 else ("q", c)].wait()

    def grad_shard(i, owner):
        value = dot(cot[...], wf[rows_at(owner * SHARD, SHARD), :], 1, 1).astype(BF16)
        gs[i] = value
        d = lax.rem(owner + 4 - x, 4)
        copy = remote(gs.at[i], gb.at[q_rows], s_gr.at[i], r_gr.at[d], device(owner, y, z, core))

        @pl.when(d == 0)
        def _():
            gb[q_rows, :] = value

        @pl.when(d != 0)
        def _():
            copy.start()

        return d, copy

    def halo_send(c, t):
        got_in(t, c)
        buf = (kb, vb)[t]
        src = buf.at[c, OWN + TOK:KEYS]
        copy = remote(src, buf.at[c, TEXT:OWN], s_halo.at[t, c], r_halo.at[t, c], super_peer(1))
        pending.append(copy)
        if t == 1 or c == 0:
            copy.start()
            return

        @pl.when(z != 7)
        def _():
            copy.start()

        @pl.when(z == 7)
        def _():
            remote(src, relf.at[c], s_halo.at[t, c], r_rf.at[c], y_peer(2)).start()

    def relay_f(c):
        @pl.when(z == 7)
        def _():
            got(relf.at[c], s_rf.at[c], r_rf.at[c])
            remote(relf.at[c], kb.at[c, TEXT:OWN], s_rf.at[c], r_halo.at[0, c], z_peer(1)).start()

    def relay_b(c):
        @pl.when(z == 0)
        def _():
            got(relb.at[c], s_rb.at[c], r_rb.at[c])
            remote(relb.at[c], hrk.at[c], s_rb.at[c], r_hb.at[0, c], z_peer(7)).start()

    def halo_got(c):
        for t, buf in enumerate((kb, vb)):
            got(buf.at[c, TEXT:OWN], s_halo.at[t, c], r_halo.at[t, c])

    own_f = yl * 2 + core
    core_f = yl * 2 + 1 - core
    y_f = (1 - yl) * 2 + core
    diag_f = (1 - yl) * 2 + 1 - core
    locals_["cot"].wait()
    locals_["w"].wait()
    grads = [grad_shard(0, own_f)]
    halo_send(0, 0)
    got(wf.at[rows_at(core_f * SHARD, SHARD)], s_w.at[2], r_w.at[2])
    grads.append(grad_shard(1, core_f))
    halo_send(0, 1)
    relay = remote(wf.at[rows_at(y_f * SHARD, SHARD)], wf.at[rows_at(y_f * SHARD, SHARD)], s_w.at[3], r_w.at[3], other_core())

    def weight_y():
        for part in (0, 1):
            got(wf.at[rows_at(y_f * SHARD + part * half, half)], s_w.at[part], r_w.at[part])
        relay.start()
        return grad_shard(2, y_f)

    def weight_diag():
        got(wf.at[rows_at(diag_f * SHARD, SHARD)], s_w.at[3], r_w.at[3])
        return grad_shard(3, diag_f)

    @pl.when(z != 0)
    def _():
        weight_y()

    halo_send(1, 0)
    halo_send(1, 1)

    @pl.when(z != 0)
    def _():
        weight_diag()

    def chunk_at(ref, c, b):
        def at(i):
            if i < 2:
                return ref[c, i * TOK:(i + 1) * TOK, :]
            return ref[c, rows_at(TEXT + (b + i - 2) * TOK, TOK), :]
        return at

    def back_copy(src, dst, ssem, rsem, c, b):
        d = lax.rem(b + 4 - x, 4)
        return remote(src, dst.at[:, head(x, c)], ssem.at[c, b], rsem.at[c, d], device(b, y, z, core))

    def forward(c, j):
        b = 3 - j
        rows = rows_at(b * TOK, TOK)
        out, inverse = forward_unit(qb[c, rows, :], chunk_at(kb, c, b), chunk_at(vb, c, b), prob.at[c * 4 + b], score)
        stat[c * 4 + b, 0:1, :] = inverse
        ob[c, rows, :] = out

        @pl.when(b == x)
        def _():
            att[:, head(x, c)] = out

        @pl.when(b != x)
        def _():
            back_copy(ob.at[c, rows], att, s_att, r_att, c, b).start()

    def backward(c, j):
        b = 3 - j
        rows = rows_at(b * TOK, TOK)

        def adder(ref):
            def add(i, value):
                at = rows_at((b + i) * TOK, TOK)
                ref[c, at, :] += value
            return add

        out = backward_unit(
            qb[c, rows, :], gb[rows, c * HEAD:(c + 1) * HEAD], ob[c, rows, :], stat[c * 4 + b, 0:1, :],
            chunk_at(kb, c, b), chunk_at(vb, c, b), prob.at[c * 4 + b], adder(dka), adder(dva))
        dqb[c, rows, :] = out

        @pl.when(b != x)
        def _():
            back_copy(dqb.at[c, rows], dq_hbm, s_dq, r_dq, c, b).start()

    def loop(fn, c, start, stop):
        def body(j, carry):
            fn(c, j)
            return carry
        lax.fori_loop(start, stop, body, 0)

    def finish(c):
        for t, (acc, recv, out, dst) in enumerate(((dka, hrk, okb, dk_hbm), (dva, hrv, ovb, dv_hbm))):
            got(recv.at[c], s_hb.at[t, c], r_hb.at[t, c])
            out[c, 0:TOK, :] = acc[c, HALO:HALO + TOK, :].astype(BF16)
            out[c, TOK:4 * TOK, :] = (acc[c, HALO + TOK:HALO + 4 * TOK, :] + recv[c].astype(F32)).astype(BF16)
            for d in (1, 3, 2):
                b = lax.rem(x + d, 4)
                send(out.at[c, rows_at(b * TOK, TOK)], dst.at[:, head(x, c)],
                     s_dkv.at[t, c, d - 1], r_dkv.at[t, c, d - 1], x_peer(d))
            local(("out", t, c), out.at[c, q_rows], dst.at[:, head(x, c)])

    def project(c):
        for d in (1, 2, 3):
            got(att.at[:, head(lax.rem(x + 4 - d, 4), c)], s_att.at[c, 0], r_att.at[c, d])
        for i in range(2):
            gsend[c, i] = dot(att[:, head(i * 2 + 1 - core, c)], cot[...], 0, 0).astype(BF16)
        send(gsend.at[c], grecv.at[c], s_c.at[c], r_c.at[c], other_core())
        for i in range(2):
            gacc[c, i] = dot(att[:, head(i * 2 + core, c)], cot[...], 0, 0)

    def y_phase(c):
        got(grecv.at[c], s_c.at[c], r_c.at[c])
        ysend[c] = (gacc[c, 1 - yl] + grecv[c, 1 - yl].astype(F32)).astype(BF16)
        for i, d in enumerate((1, 3)):
            at = slice(i * 64, (i + 1) * 64)
            send(ysend.at[c, at], yrecv.at[c, at], s_y.at[c, i], r_y.at[c, i], y_peer(d))
        gsum[c * HEAD:(c + 1) * HEAD, :] = gacc[c, yl] + grecv[c, yl].astype(F32)

    def y_merge(c):
        for i in range(2):
            got(yrecv.at[c, i * 64:(i + 1) * 64], s_y.at[c, i], r_y.at[c, i])
        gsum[c * HEAD:(c + 1) * HEAD, :] += yrecv[c].astype(F32)

    def h_copy(h):
        return remote(hsend.at[h], hrecv.at[h], s_h.at[h], r_h.at[h], y_peer(2))

    def h_phase():
        for h in range(2):
            hsend[h] = gsum[rows_at((1 - yh) * 192 + h * 96, 96), :].astype(BF16)
            h_copy(h).start()

    def z_copy(t):
        d = lax.rem(t + 8 - z, 8)
        return remote(zsend.at[t], zrecv.at[d], s_z.at[t], r_z.at[d], device(x, y, t, core))

    def z_phase(h):
        got(hrecv.at[h], s_h.at[h], r_h.at[h])
        yown[h * 96:(h + 1) * 96, :] = gsum[rows_at(yh * 192 + h * 96, 96), :] + hrecv[h].astype(F32)
        for t in range(4 * h, 4 * h + 4):
            zsend[t] = yown[t * 24:(t + 1) * 24, :].astype(BF16)

            @pl.when(z != t)
            def _(t=t):
                z_copy(t).start()

    def x_phase():
        total = yown[pl.ds(pl.multiple_of(z * 24, 8), 24), :]
        for d in range(1, 8):
            got(zrecv.at[d], s_z.at[d], r_z.at[d])
            total = total + zrecv[d].astype(F32)
        for i in range(4):
            xsend[i] = total[i * 6:(i + 1) * 6]
        for d in (2, 1, 3):
            send(xsend.at[lax.rem(x + d, 4)], xrecv.at[d - 1], s_x.at[d - 1], r_x.at[d - 1], x_peer(d))

    def x_done():
        total = xsend[x]
        for d in range(1, 4):
            got(xrecv.at[d - 1], s_x.at[d - 1], r_x.at[d - 1])
            total = total + xrecv[d - 1]
        gw_ref[...] = total

    def image():
        for n in range(3):
            at = slice(n * 512, (n + 1) * 512)
            img[:, at] = dot(att[...], wf[:, at], 1, 0).astype(BF16)
        local("img", img, img_hbm)

    def forward_chunk(c):
        got_in(2, c)
        locals_[("tk", c)].wait()
        locals_[("tv", c)].wait()
        halo_got(c)
        loop(forward, c, 0, 4)

    def backward_end(c):
        local(("dq", c), dqb.at[c, q_rows], dq_hbm.at[:, head(x, c)])
        for t, (acc, out, recv) in enumerate(((dka, hsk, hrk), (dva, hsv, hrv))):
            out[c] = acc[c, 0:HALO, :].astype(BF16)
            copy = remote(out.at[c], recv.at[c], s_hb.at[t, c], r_hb.at[t, c], super_peer(15))
            pending.append(copy)
            if t == 1:
                copy.start()
                continue

            @pl.when(z != 0)
            def _(copy=copy):
                copy.start()

            @pl.when(z == 0)
            def _(out=out, t=t):
                remote(out.at[c], relb.at[c], s_hb.at[t, c], r_rb.at[c], y_peer(2)).start()

    forward_chunk(0)
    halo_send(2, 0)
    relay_f(1)
    halo_send(2, 1)

    @pl.when(z == 0)
    def _():
        weight_y()

    forward_chunk(1)
    relay_f(2)

    @pl.when(z == 0)
    def _():
        weight_diag()

    forward_chunk(2)
    for i, owner in ((2, y_f), (3, diag_f)):
        d = lax.rem(owner + 4 - x, 4)
        grads.append((d, remote(gs.at[i], gb.at[q_rows], s_gr.at[i], r_gr.at[d], device(owner, y, z, core))))
    pending.append(relay)
    for d in (1, 2, 3):
        got(gb.at[rows_at(lax.rem(x + 4 - d, 4) * TOK, TOK)], s_gr.at[0], r_gr.at[d])
    loop(backward, 0, 0, 2)
    project(0)
    loop(backward, 0, 2, 4)
    backward_end(0)
    project(1)
    y_phase(0)
    project(2)
    loop(backward, 1, 0, 1)
    y_phase(1)
    loop(backward, 1, 1, 2)
    y_phase(2)
    loop(backward, 1, 2, 4)
    backward_end(1)
    relay_b(0)
    loop(backward, 2, 0, 2)

    def merge():
        for c in range(3):
            y_merge(c)
        h_phase()

    @pl.when(z != 0)
    def _():
        merge()

    loop(backward, 2, 2, 4)
    backward_end(2)
    relay_b(1)

    @pl.when(z == 0)
    def _():
        merge()

    for h in range(2):
        pending.append(h_copy(h))
    finish(0)
    image()
    relay_b(2)
    finish(1)
    z_phase(0)
    z_phase(1)
    finish(2)
    x_phase()
    for c in range(3):
        for d in (1, 2, 3):
            cols = head(lax.rem(x + 4 - d, 4), c)
            got(dq_hbm.at[:, cols], s_dq.at[c, 0], r_dq.at[c, d])
            got(dk_hbm.at[:, cols], s_dkv.at[0, c, d - 1], r_dkv.at[0, c, d - 1])
            got(dv_hbm.at[:, cols], s_dkv.at[1, c, d - 1], r_dkv.at[1, c, d - 1])
    x_done()

    for copy in pending:
        copy.wait_send()
    for d, copy in grads:
        @pl.when(d != 0)
        def _(copy=copy):
            copy.wait_send()
    for t in range(8):
        @pl.when(z != t)
        def _(t=t):
            z_copy(t).wait_send()
    for c in (1, 2):
        @pl.when(z == 7)
        def _(c=c):
            remote(relf.at[c], kb.at[c, TEXT:OWN], s_rf.at[c], r_halo.at[0, c], z_peer(1)).wait_send()

    for c in range(3):
        @pl.when(z == 0)
        def _(c=c):
            remote(relb.at[c], hrk.at[c], s_rb.at[c], r_hb.at[0, c], z_peer(7)).wait_send()
    locals_["img"].wait()
    for c in range(3):
        locals_[("dq", c)].wait()
        for t in range(2):
            locals_[("out", t, c)].wait()
        for b in range(4):
            @pl.when(b != x)
            def _(c=c, b=b):
                rows = pl.ds(b * TOK, TOK)
                back_copy(ob.at[c, rows], att, s_att, r_att, c, b).wait_send()
                back_copy(dqb.at[c, rows], dq_hbm, s_dq, r_dq, c, b).wait_send()


def per_device(image_query, image_key, image_value, text_key, text_value, out_weight, cotangent):
    any_ = pl.BlockSpec(memory_space=pl.ANY)
    vmem = pl.BlockSpec(memory_space=pltpu.VMEM)
    dma = pltpu.SemaphoreType.DMA
    block = jax.ShapeDtypeStruct((TOK, INNER), BF16)
    V = pltpu.VMEM
    img, dq, dk, dv, gw = pl.pallas_call(
        kernel,
        out_shape=(block, block, block, block, jax.ShapeDtypeStruct((6, INNER), F32)),
        in_specs=[any_] * 7,
        out_specs=(any_, any_, any_, any_, vmem),
        scratch_shapes=[
            V((TOK, INNER), BF16), V((TOK, INNER), BF16), V((INNER, INNER), BF16),
            V((3, KEYS, HEAD), BF16), V((3, KEYS, HEAD), BF16), V((3, 4 * TOK, HEAD), BF16),
            V((4, TOK, SHARD), BF16), V((4 * TOK, SHARD), BF16),
            V((12, 6, TOK, TOK), BF16), V((6, TOK, TOK), F32), V((12, 8, TOK), F32),
            V((3, 4 * TOK, HEAD), BF16), V((3, 4 * TOK, HEAD), BF16), V((TOK, INNER), BF16),
            V((3, 7 * TOK, HEAD), F32), V((3, 7 * TOK, HEAD), F32),
            V((3, HALO, HEAD), BF16), V((3, HALO, HEAD), BF16), V((3, HALO, HEAD), BF16), V((3, HALO, HEAD), BF16),
            V((3, 4 * TOK, HEAD), BF16), V((3, 4 * TOK, HEAD), BF16),
            V((3, HALO, HEAD), BF16), V((3, HALO, HEAD), BF16),
            V((3, 2, HEAD, INNER), F32), V((3, 2, HEAD, INNER), BF16), V((3, 2, HEAD, INNER), BF16),
            V((3, HEAD, INNER), BF16), V((3, HEAD, INNER), BF16), V((SHARD, INNER), F32),
            V((2, 96, INNER), BF16), V((2, 96, INNER), BF16), V((192, INNER), F32),
            V((8, 24, INNER), BF16), V((8, 24, INNER), BF16), V((4, 6, INNER), F32), V((3, 6, INNER), F32),
            dma((32,)), dma((3, 3, 3)), dma((3, 3, 3)), dma((4,)), dma((4,)), dma((4,)), dma((4,)),
            dma((2, 3)), dma((2, 3)),
            dma((3,)), dma((3,)), dma((3,)), dma((3,)),
            dma((3, 4)), dma((3, 4)), dma((3, 4)), dma((3, 4)), dma((2, 3, 3)), dma((2, 3, 3)),
            dma((2, 3)), dma((2, 3)),
            dma((3,)), dma((3,)), dma((3, 2)), dma((3, 2)), dma((2,)), dma((2,)), dma((8,)), dma((8,)), dma((3,)), dma((3,)),
        ],
        compiler_params=pltpu.CompilerParams(
            collective_id=0, has_side_effects=True, vmem_limit_bytes=62 * 1024 * 1024
        ),
    )(image_query[0], image_key[0], image_value[0], text_key[0], text_value[0], out_weight, cotangent[0])
    return img[None], dq[None], dk[None], dv[None], gw


def solution(mesh):
    part = P("fsdp", "seq", None)
    text = P("fsdp", None, None)
    return jax.shard_map(
        per_device, mesh=mesh,
        in_specs=(part, part, part, text, text, P("fsdp", None), part),
        out_specs=(part, part, part, part, P(("fsdp", "seq"), None)),
        check_vma=False,
    )
```

time: 819 us -> 121 us (0.15)
  blocking collectives: 298 us -> 0 us
  waiting for transfers between devices: 201 us -> 0 us
  matrix products: 124 us -> 0 us
  starting transfers between devices: 115 us -> 0 us
  Pallas kernels: 0 us -> 113 us
  local copies, waits for them, and re-layouts: 49.5 us -> 5.45 us
  between operations: 15.3 us -> 0.66 us
  other arithmetic: 13.1 us -> 0 us
    unnamed x1 -> x0, blocking collectives: 298 us -> none
    ppermute x12 -> x0, waiting for transfers between devices: 200 us -> none  [from_behind(): return lax.ppermute(block, axis, route)]
    dot_general x75 -> x0, matrix products: 124 us -> none  [the longest x12 24.2 us: head_pass(): lax.dot_general(grad_score, head_query, (((0,), (0,)), ((), ())), preferr...]
    pallas_call x0 -> x1, Pallas kernels: none -> 113 us  [per_device(): pl.pallas_call(kernel, out_shape=(block, block, block, block, jax.ShapeDt...]
    ppermute x12 -> x0, starting transfers between devices: 59.2 us -> none  [from_behind(): return lax.ppermute(block, axis, route)]
    unnamed x16 -> x0, starting transfers between devices: 55.6 us -> none
    unnamed x60 -> x13, local copies, waits for them, and re-layouts: 31.3 us -> 5.45 us
    dynamic_update_slice x24 -> x0, local copies, waits for them, and re-layouts: 8.96 us -> none  [per_device(): lax.map(head_pass, (split_heads(queries, HEAD_DIM), split_heads(set_keys,...]
  transfers between devices with their start and end apart: 30 -> 0, of which waited for: 10 -> 0; matrix products, arithmetic and copies ran while one was open for 43% -> 0% of each run, Pallas kernels for 0% -> 0%
where the time goes in v1:
time: 121 us; the launch traced here: 120 us
  Pallas kernels  113 us (93%)
  local copies, waits for them, and re-layouts  5.45 us (5%)
    pallas_call x1, Pallas kernels, per_device(): pl.pallas_call(kernel, out_shape=(block, block, block, block, jax.ShapeDt...  113 us
    unnamed x13, local copies, waits for them, and re-layouts  5.45 us

profile of v1, /device:TPU:2, one launch (start us, length us, event | category | flops | bytes accessed | tf_op | source)
XLA Modules:
  0.0 119.6 jit_solution(916942212003777551)
XLA Ops:
  0.6 113.5 %shard_map.110 = (bf16[256,1536]{1,0:T(8,128)(2,1)}, bf16[256,1536]{1,0:T(8,128)(2,1)}, bf16[256,1536]{1,0:T(8,128)(2,1)}, bf16[256,1536]{1,0:T(8,128)(2,1)}, f32[6,1536]{1,0:T(8,128)}) custom-call(bf16[256,1536]{1,0:T(8,128)(2,1)} %bitcast.12, bf16[256,1536]{1,0:T(8,128)(2,1)} %bitcast.13, bf16[256,1536]{1,0:T(8,128)(2,1)} %bitcast.14, ...), custom_call_target="tpu_custom_call" | custom-call | tf_op jit(solution)/shard_map/pallas_call | solution.py:531
  114.1 0.0 copy-start.2
  114.1 0.0 copy-start.1
  114.1 2.2 %copy.17 = bf16[1,256,1536]{2,1,0:T(8,128)(2,1)} copy(bf16[1,256,1536]{2,1,0:T(8,128)(2,1)} %bitcast.19) | data formatting | bytes 1572864
  116.3 0.0 copy-done.2
  116.3 0.0 copy-start
  116.3 0.9 copy.18
  117.2 0.0 copy-done.1
  117.2 0.0 copy-start.3
  117.2 0.9 copy.19
  118.1 0.0 copy-done
  118.1 0.9 copy.20
  119.0 0.0 copy-done.3
  119.0 0.6 copy.21
Async XLA Ops:
  114.1 2.2 %copy-start.2 = (bf16[256,1536]{1,0:T(8,128)(2,1)S(1)}, bf16[256,1536]{1,0:T(8,128)(2,1)}, u32[]{:S(2)}) copy-start(bf16[256,1536]{1,0:T(8,128)(2,1)} %get-tuple-element.11) | copy-start | bytes 2359300
  114.1 3.1 %copy-start.1 = (bf16[256,1536]{1,0:T(8,128)(2,1)S(1)}, bf16[256,1536]{1,0:T(8,128)(2,1)}, u32[]{:S(2)}) copy-start(bf16[256,1536]{1,0:T(8,128)(2,1)} %get-tuple-element.12) | copy-start | bytes 2359300
  116.3 1.8 %copy-start = (bf16[256,1536]{1,0:T(8,128)(2,1)S(1)}, bf16[256,1536]{1,0:T(8,128)(2,1)}, u32[]{:S(2)}) copy-start(bf16[256,1536]{1,0:T(8,128)(2,1)} %get-tuple-element.13) | copy-start | bytes 2359300
  117.2 1.8 %copy-start.3 = (f32[6,1536]{1,0:T(8,128)S(1)}, f32[6,1536]{1,0:T(8,128)}, u32[]{:S(2)}) copy-start(f32[6,1536]{1,0:T(8,128)} %get-tuple-element.24) | copy-start | bytes 110596
